TPU v7x, 32 devices: a whole 2x2x4 slice. The times are simulated.
32 devices in a mesh: au: 4 (over y, x), vert: 8 (over z, core).
Axes of the slice: x: 2, y: 2, z: 4, core: 2. Of those that a mesh axis runs over, the one named last changes fastest.
Arguments:
- visibility: bfloat16 [2, 65536], P(None, ('au', 'vert')), may hold values from -6 to 6
- taps_u: bfloat16 [16, 65536], P(None, ('au', 'vert')), may hold values from 0.019897461 to 0.44921875
- taps_v: bfloat16 [16, 65536], P(None, ('au', 'vert')), may hold values from 0.019897461 to 0.44921875
- facet: int32 [65536, 1], P(('au', 'vert')), may hold values from 0 to 31; in each aligned block of 2048 rows (0 to 2047, 2048 to 4095, ...) at most 256 rows name the same one
- u_offset: int32 [65536], P(('au', 'vert')), may hold values from 0 to 2032
- v_offset: int32 [65536], P(('au', 'vert')), may hold values from 0 to 1008
Outputs:
- image: float32 [2, 8192, 8192], P(None, ('au', 'vert'))
Inputs may be any that keep to these rules, and one draw needn't show every extreme that they name: Of the 2048 visibilities of one device at most 256 name the same facet, and some facet gets exactly 256 of some device's visibilities.
All inputs are finite; a program needn't handle non-finite values.
Results may differ from a plain program's by a relative error of at most 0.0058.
Values may be sent and summed in bfloat16 or wider, within the bound.
A program may use at most 128 MiB of HBM per device.

v0:
```python
import math

import jax
import jax.numpy as jnp
from jax import lax
from jax.sharding import PartitionSpec as P

GRID = 8192
TAPS = 16


highest = lax.Precision.HIGHEST


def split_length(length):
    first = 1
    trial = 1
    while trial * trial <= length:
        if length % trial == 0:
            first = trial
        trial = trial + 1
    return (first, length // first)


def angle_table(rows, cols, modulus):
    product = (
        jnp.arange(rows, dtype=jnp.int32)[:, None]
        * jnp.arange(cols, dtype=jnp.int32)[None, :]
        % modulus
    )
    phase = product.astype(jnp.float32) * (2.0 * math.pi / modulus)
    return (jnp.cos(phase), jnp.sin(phase))


def complex_einsum(form, left_re, left_im, right_re, right_im):
    real_part = jnp.einsum(form, left_re, right_re, precision=highest) - jnp.einsum(
        form, left_im, right_im, precision=highest
    )
    imag_part = jnp.einsum(form, left_re, right_im, precision=highest) + jnp.einsum(
        form, left_im, right_re, precision=highest
    )
    return (real_part, imag_part)


def transform_last(values, final_form):
    length = values.shape[2]
    first, second = split_length(length)
    items = values.shape[1]
    real_in = values[0].reshape(items, first, second)
    imag_in = values[1].reshape(items, first, second)
    outer_cos, outer_sin = angle_table(first, first, first)
    inner_cos, inner_sin = angle_table(second, second, second)
    twist_cos, twist_sin = angle_table(first, second, length)
    mid_re, mid_im = complex_einsum("mab,ak->mkb", real_in, imag_in, outer_cos, outer_sin)
    turned_re = mid_re * twist_cos - mid_im * twist_sin
    turned_im = mid_re * twist_sin + mid_im * twist_cos
    return complex_einsum(final_form, turned_re, turned_im, inner_cos, inner_sin)


def columns_transform(values):
    out_re, out_im = transform_last(values, "mkb,bj->jkm")
    length = values.shape[2]
    items = values.shape[1]
    return jnp.stack([out_re.reshape(length, items), out_im.reshape(length, items)])


def rows_transform(values):
    out_re, out_im = transform_last(values, "mkb,bj->mjk")
    length = values.shape[2]
    items = values.shape[1]
    return jnp.stack([out_re.reshape(items, length), out_im.reshape(items, length)])


def first_columns(values):
    return columns_transform(values[:, 0])


def band_matrix(gap, weight_of):
    zero = jnp.zeros((), jnp.bfloat16)
    matrix = jnp.where(gap == 0, weight_of(0), zero)
    for tap_index in range(1, TAPS):
        matrix = matrix + jnp.where(gap == tap_index, weight_of(tap_index), zero)
    return matrix


def on_device(visibility, taps_u, taps_v, facet, u_offset, v_offset):
    n_au = lax.axis_size("au")
    n_vert = lax.axis_size("vert")
    devices = n_au * n_vert
    rows_u = GRID // n_au
    cols_v = GRID // n_vert
    count = visibility.shape[1]
    capacity = max(2, 4 * count // devices)
    target = facet[:, 0]
    onehot = (target[:, None] == jnp.arange(devices, dtype=jnp.int32)[None, :]).astype(jnp.int32)
    rank = jnp.sum(onehot * (jnp.cumsum(onehot, axis=0) - 1), axis=1)
    slot = target * capacity + rank
    kv = taps_v.astype(jnp.float32)
    weighted_re = (visibility[0:1].astype(jnp.float32) * kv).astype(jnp.bfloat16)
    weighted_im = (visibility[1:2].astype(jnp.float32) * kv).astype(jnp.bfloat16)
    payload = jnp.concatenate([taps_u, weighted_re, weighted_im], axis=0)
    fields = payload.shape[0]
    packed = jnp.zeros((fields, devices * capacity), jnp.bfloat16).at[:, slot].set(payload)
    placed = jnp.zeros((devices * capacity,), jnp.int32).at[slot].set(u_offset * cols_v + v_offset)
    packed = packed.reshape(fields, n_au, n_vert, capacity)
    placed = placed.reshape(1, n_au, n_vert, capacity)
    arrived, spots = (
        lax.all_to_all(
            lax.all_to_all(packed, "au", split_axis=1, concat_axis=1, tiled=True),
            "vert",
            split_axis=2,
            concat_axis=2,
            tiled=True,
        ),
        lax.all_to_all(
            lax.all_to_all(placed, "au", split_axis=1, concat_axis=1, tiled=True),
            "vert",
            split_axis=2,
            concat_axis=2,
            tiled=True,
        ),
    )
    total = devices * capacity
    arrived = arrived.reshape(fields, total)
    spots = spots.reshape(total)
    block = math.gcd(total, 2048)

    def grid_block(step, acc):
        start = step * block
        piece = lax.dynamic_slice_in_dim(arrived, start, block, 1)
        spot = lax.dynamic_slice_in_dim(spots, start, block, 0)
        row_start = spot // cols_v
        col_start = spot % cols_v
        row_gap = jnp.arange(rows_u, dtype=jnp.int32)[None, :] - row_start[:, None]
        row_weights = jnp.transpose(piece[0:TAPS])
        u_matrix = band_matrix(row_gap, lambda t: row_weights[:, t : t + 1])
        col_gap = jnp.arange(cols_v, dtype=jnp.int32)[:, None] - col_start[None, :]
        v_real = band_matrix(col_gap, lambda t: piece[TAPS + t : TAPS + t + 1])
        v_imag = band_matrix(col_gap, lambda t: piece[2 * TAPS + t : 2 * TAPS + t + 1])
        v_matrix = jnp.concatenate([v_real, v_imag], axis=0)
        return acc + jnp.dot(v_matrix, u_matrix, preferred_element_type=jnp.float32)

    empty = jnp.zeros((2 * cols_v, rows_u), jnp.float32)
    grid = lax.fori_loop(0, total // block, grid_block, empty)
    grid = grid.reshape(2, n_au, cols_v // n_au, rows_u)
    turned = first_columns(lax.all_to_all(grid, "au", split_axis=1, concat_axis=3, tiled=True))
    band = rows_u // n_vert
    sectioned = turned.reshape(2, n_au, n_vert, band, turned.shape[2])
    joined = lax.all_to_all(
        lax.all_to_all(sectioned, "au", split_axis=1, concat_axis=4, tiled=True),
        "vert",
        split_axis=2,
        concat_axis=4,
        tiled=True,
    )
    picture = rows_transform(joined.reshape(2, band, GRID))
    return picture * (1.0 / math.sqrt(count * devices))


def solution(mesh):
    return jax.shard_map(
        on_device,
        mesh=mesh,
        in_specs=(
            P(None, ("au", "vert")),
            P(None, ("au", "vert")),
            P(None, ("au", "vert")),
            P(("au", "vert"), None),
            P(("au", "vert")),
            P(("au", "vert")),
        ),
        out_specs=P(None, ("au", "vert"), None),
        check_vma=False,
    )
```

profile of v0, /device:TPU:0, one launch (start us, length us, event | category | flops | bytes accessed | tf_op | source)
XLA Modules:
  0.0 1614.8 jit_solution(12085499914736727891)
XLA Ops:
  66.5 20.8 %all-to-all-done.3 = bf16[48,4,8,256]{3,0,1,2:T(8,128)(2,1)S(1)} async-done(((bf16[48,4,8,256]{3,0,1,2:T(8,128)(2,1)}), bf16[48,4,8,256]{3,0,1,2:T(8,128)(2,1)S(1)}, u32[]{:S(2)}, u32[]{:S(2)}) %all-to-all-start.3) | async-done | bytes 786464 | tf_op jit(solution)/shard_map/all_to_all | solution.py:108
  88.2 360.5 %while.16 = (s32[]{:T(128)}, f32[2048,2048]{1,0:T(8,128)}, s32[8192]{0:T(1024)S(1)}, bf16[48,8192]{1,0:T(8,128)(2,1)S(1)}, s32[]{:T(128)}, /*index=5*/s32[]{:T(1...) while((s32[]{:T(128)}, f32[2048,2048]{1,0:T(8,128)}, ...), condition=%wide.region_6.7_spmd.clone, body=%wide.region_5.6_spmd.clone.sunk | while | flops 17750345728 | bytes 67892128 | solution.py:144
  88.7 34.8 %fusion.389 = bf16[2048,2048]{1,0:T(8,128)(2,1)} fusion(s32[2048]{0:T(1024)S(1)} %get-tuple-element.314, bf16[2048]{0:T(1024)(128)(2,1)S(1)} %get-tuple-element.315, bf16[2048]{0:T(1024)(128)(2,1)S(1)} %get-tuple-element.316, bf16[2048]{0:T(1024)(128)(2,1)S(1)} %get-tuple-element.317, bf16[2048]{0:T(1024)(128)(2,1)S(1)} %get-tuple-element.318, ...), kind=kLoop, calls=%fused_computation.36.clone.clone.2.clone.1 | loop fusion | flops 272629760 | bytes 8462336 | tf_op jit(solution)/shard_map/while/body/eval_jaxpr/dot_general | solution.py:141
  124.5 14.4 fusion.388
  138.9 14.3 fusion.387
  153.2 24.3 %select_add_fusion.2 = f32[2048,2048]{1,0:T(8,128)} fusion(f32[2048,2048]{1,0:T(8,128)} %get-tuple-element.372, bf16[1024,2048]{1,0:T(8,128)(2,1)} %fusion.387, bf16[1024,2048]{1,0:T(8,128)(2,1)} %fusion.388, pred[]{:T(512)S(6)} %compare.22, bf16[2048,2048]{1,0:T(8,128)(2,1)} %fusion.389), kind=kOutput, calls=%fused_computation.2.clone.3 | convolution fusion | flops 17205035008 | bytes 50331648 | tf_op jit(solution)/shard_map/while/body/eval_jaxpr/dot_general | solution.py:141
  177.9 34.8 %fusion.389 = bf16[2048,2048]{1,0:T(8,128)(2,1)} fusion(s32[2048]{0:T(1024)S(1)} %get-tuple-element.314, bf16[2048]{0:T(1024)(128)(2,1)S(1)} %get-tuple-element.315, bf16[2048]{0:T(1024)(128)(2,1)S(1)} %get-tuple-element.316, bf16[2048]{0:T(1024)(128)(2,1)S(1)} %get-tuple-element.317, bf16[2048]{0:T(1024)(128)(2,1)S(1)} %get-tuple-element.318, ...), kind=kLoop, calls=%fused_computation.36.clone.clone.2.clone.1 | loop fusion | flops 272629760 | bytes 8462336 | tf_op jit(solution)/shard_map/while/body/eval_jaxpr/dot_general | solution.py:141
  213.7 14.4 fusion.388
  228.1 14.3 fusion.387
  242.4 25.5 %select_add_fusion.2 = f32[2048,2048]{1,0:T(8,128)} fusion(f32[2048,2048]{1,0:T(8,128)} %get-tuple-element.372, bf16[1024,2048]{1,0:T(8,128)(2,1)} %fusion.387, bf16[1024,2048]{1,0:T(8,128)(2,1)} %fusion.388, pred[]{:T(512)S(6)} %compare.22, bf16[2048,2048]{1,0:T(8,128)(2,1)} %fusion.389), kind=kOutput, calls=%fused_computation.2.clone.3 | convolution fusion | flops 17205035008 | bytes 50331648 | tf_op jit(solution)/shard_map/while/body/eval_jaxpr/dot_general | solution.py:141
  268.3 34.8 %fusion.389 = bf16[2048,2048]{1,0:T(8,128)(2,1)} fusion(s32[2048]{0:T(1024)S(1)} %get-tuple-element.314, bf16[2048]{0:T(1024)(128)(2,1)S(1)} %get-tuple-element.315, bf16[2048]{0:T(1024)(128)(2,1)S(1)} %get-tuple-element.316, bf16[2048]{0:T(1024)(128)(2,1)S(1)} %get-tuple-element.317, bf16[2048]{0:T(1024)(128)(2,1)S(1)} %get-tuple-element.318, ...), kind=kLoop, calls=%fused_computation.36.clone.clone.2.clone.1 | loop fusion | flops 272629760 | bytes 8462336 | tf_op jit(solution)/shard_map/while/body/eval_jaxpr/dot_general | solution.py:141
  304.1 14.4 fusion.388
  318.5 14.3 fusion.387
  332.8 25.5 %select_add_fusion.2 = f32[2048,2048]{1,0:T(8,128)} fusion(f32[2048,2048]{1,0:T(8,128)} %get-tuple-element.372, bf16[1024,2048]{1,0:T(8,128)(2,1)} %fusion.387, bf16[1024,2048]{1,0:T(8,128)(2,1)} %fusion.388, pred[]{:T(512)S(6)} %compare.22, bf16[2048,2048]{1,0:T(8,128)(2,1)} %fusion.389), kind=kOutput, calls=%fused_computation.2.clone.3 | convolution fusion | flops 17205035008 | bytes 50331648 | tf_op jit(solution)/shard_map/while/body/eval_jaxpr/dot_general | solution.py:141
  358.7 34.8 %fusion.389 = bf16[2048,2048]{1,0:T(8,128)(2,1)} fusion(s32[2048]{0:T(1024)S(1)} %get-tuple-element.314, bf16[2048]{0:T(1024)(128)(2,1)S(1)} %get-tuple-element.315, bf16[2048]{0:T(1024)(128)(2,1)S(1)} %get-tuple-element.316, bf16[2048]{0:T(1024)(128)(2,1)S(1)} %get-tuple-element.317, bf16[2048]{0:T(1024)(128)(2,1)S(1)} %get-tuple-element.318, ...), kind=kLoop, calls=%fused_computation.36.clone.clone.2.clone.1 | loop fusion | flops 272629760 | bytes 8462336 | tf_op jit(solution)/shard_map/while/body/eval_jaxpr/dot_general | solution.py:141
  394.5 14.4 fusion.388
  408.9 14.3 fusion.387
  423.2 25.5 %select_add_fusion.2 = f32[2048,2048]{1,0:T(8,128)} fusion(f32[2048,2048]{1,0:T(8,128)} %get-tuple-element.372, bf16[1024,2048]{1,0:T(8,128)(2,1)} %fusion.387, bf16[1024,2048]{1,0:T(8,128)(2,1)} %fusion.388, pred[]{:T(512)S(6)} %compare.22, bf16[2048,2048]{1,0:T(8,128)(2,1)} %fusion.389), kind=kOutput, calls=%fused_computation.2.clone.3 | convolution fusion | flops 17205035008 | bytes 50331648 | tf_op jit(solution)/shard_map/while/body/eval_jaxpr/dot_general | solution.py:141
  467.7 182.1 %all-to-all-done.4 = f32[2,4,256,2048]{3,2,0,1:T(8,128)} async-done(((f32[2,4,256,2048]{3,2,0,1:T(8,128)}), f32[2,4,256,2048]{3,2,0,1:T(8,128)}, u32[]{:S(2)}, u32[]{:S(2)}) %all-to-all-start.4) | async-done | bytes 16777248 | tf_op jit(solution)/shard_map/all_to_all | solution.py:146
  741.3 19.6 %subtract_bitcast_fusion.3 = (f32[256,64,128]{2,1,0:T(8,128)}, f32[256,64,128]{2,1,0:T(8,128)}) fusion(f32[64,128]{1,0:T(8,128)S(1)} %get-tuple-element.204, f32[64,128]{1,0:T(8,128)S(1)} %get-tuple-element.205, f32[64,256,128]{2,0,1:T(8,128)} %fusion.252, f32[64,256,128]{2,0,1:T(8,128)} %fusion.260, f32[64,256,128]{2,0,1:T(8,128)} %fusion.254, ...), kind=kOutput, calls=%fused_computation.252 | convolution fusion | flops 1627447296 | bytes 50397184 | tf_op jit(solution)/shard_map/mab,ak->mkb/dot_general | solution.py:36
  761.0 18.4 %fusion.207 = f32[128,256,64]{1,0,2:T(8,128)} fusion(f32[256,64,128]{2,1,0:T(8,128)} %get-tuple-element.195), kind=kOutput, calls=%fused_computation.263 | convolution fusion | flops 3221454848 | bytes 16777216 | tf_op jit(solution)/shard_map/mkb,bj->jkm/dot_general | solution.py:36
  779.4 13.0 fusion.205
  792.4 19.3 %subtract_bitcast_fusion.2 = f32[128,64,256]{2,0,1:T(8,128)} fusion(f32[128,256,64]{1,0,2:T(8,128)} %fusion.207, f32[256,64,128]{2,1,0:T(8,128)S(1)} %bitcast.123), kind=kOutput, calls=%fused_computation.250 | convolution fusion | flops 3223552000 | bytes 25165824 | tf_op jit(solution)/shard_map/mkb,bj->jkm/dot_general | solution.py:36
  823.2 17.8 %add_bitcast_fusion.2 = f32[128,64,256]{2,0,1:T(8,128)} fusion(f32[128,256,64]{1,0,2:T(8,128)S(1)} %fusion.205, f32[256,64,128]{2,1,0:T(8,128)S(1)} %bitcast.123), kind=kOutput, calls=%fused_computation.249 | convolution fusion | flops 3223552000 | bytes 25165824 | tf_op jit(solution)/shard_map/mkb,bj->jkm/dot_general | solution.py:39
  852.5 186.6 %all_to_all.68 = f32[2,4,8,256,256]{4,3,2,0,1:T(8,128)} all-to-all(f32[2,4,8,256,256]{4,3,2,0,1:T(8,128)S(1)} %copy.100), channel_id=1, replica_groups=mesh['au'=4,'vert'=8] {'au'}, dimensions={1} | all-to-all | bytes 33554432 | tf_op jit(solution)/shard_map/all_to_all | solution.py:150
  1039.1 17.4 %copy.113 = f32[2,4,8,256,256]{3,4,1,0,2:T(8,128)} copy(f32[2,4,8,256,256]{4,3,2,0,1:T(8,128)} %all_to_all.68) | data formatting | bytes 33554432 | tf_op jit(solution)/shard_map/all_to_all | solution.py:150
  1056.5 368.2 %all_to_all.69 = f32[2,1,8,256,1024]{3,4,0,1,2:T(8,128)S(1)} all-to-all(f32[2,1,8,256,1024]{3,4,0,1,2:T(8,128)} %bitcast.125), channel_id=1, replica_groups=mesh['au'=4,'vert'=8] {'vert'}, dimensions={2} | all-to-all | bytes 33554432 | tf_op jit(solution)/shard_map/all_to_all | solution.py:149
  1482.9 19.5 %subtract_bitcast_fusion.1 = (f32[256,64,128]{2,1,0:T(8,128)}, f32[256,64,128]{2,1,0:T(8,128)}) fusion(f32[64,128]{1,0:T(8,128)S(1)} %get-tuple-element.204, f32[64,128]{1,0:T(8,128)S(1)} %get-tuple-element.205, f32[64,256,128]{2,0,1:T(8,128)} %fusion.248, f32[64,256,128]{2,0,1:T(8,128)} %fusion.256, f32[64,256,128]{2,0,1:T(8,128)} %fusion.250, ...), kind=kOutput, calls=%fused_computation.248 | convolution fusion | flops 1627447296 | bytes 50397184 | tf_op jit(solution)/shard_map/mab,ak->mkb/dot_general | solution.py:36
  1502.5 18.6 %fusion.199 = f32[128,256,64]{1,0,2:T(8,128)} fusion(f32[256,64,128]{2,1,0:T(8,128)} %get-tuple-element.193), kind=kOutput, calls=%fused_computation.255 | convolution fusion | flops 3221454848 | bytes 16777216 | tf_op jit(solution)/shard_map/mkb,bj->mjk/dot_general | solution.py:36
  1534.1 19.3 %subtract_bitcast_fusion = f32[256,128,64]{0,1,2:T(8,128)} fusion(f32[128,256,64]{1,0,2:T(8,128)} %fusion.199, f32[256,64,128]{2,1,0:T(8,128)S(1)} %bitcast.121), kind=kOutput, calls=%fused_computation.246 | convolution fusion | flops 3223552000 | bytes 25165824 | tf_op jit(solution)/shard_map/mkb,bj->mjk/dot_general | solution.py:36
  1564.9 17.8 %add_bitcast_fusion = f32[256,128,64]{0,1,2:T(8,128)} fusion(f32[128,256,64]{1,0,2:T(8,128)S(1)} %fusion.197, f32[256,64,128]{2,1,0:T(8,128)S(1)} %bitcast.121), kind=kOutput, calls=%fused_computation.245 | convolution fusion | flops 3223552000 | bytes 25165824 | tf_op jit(solution)/shard_map/mkb,bj->mjk/dot_general | solution.py:39
  1597.1 17.5 %copy.111 = f32[2,256,8192]{2,1,0:T(8,128)} copy(f32[2,256,8192]{1,2,0:T(8,128)} %maximum_multiply_fusion) | data formatting | bytes 33554432 | tf_op jit(solution)/shard_map/mul | solution.py:157
  (102 shorter events, 303.4 us)
Async XLA Ops:
  21.5 16.2 %all-to-all-start = ((s32[1,4,8,256]{3,2,0,1:T(8,128)}), s32[1,4,8,256]{3,2,0,1:T(8,128)S(1)}, u32[]{:S(2)}, u32[]{:S(2)}) async-start(s32[1,4,8,256]{3,2,0,1:T(8,128)} %reshape.89), calls=%async_computation | async-start | bytes 65536 | tf_op jit(solution)/shard_map/all_to_all | solution.py:116
  37.7 14.5 all-to-all-start.2
  52.1 10.6 all-to-all-start.1
  62.8 24.6 %all-to-all-start.3 = ((bf16[48,4,8,256]{3,0,1,2:T(8,128)(2,1)}), bf16[48,4,8,256]{3,0,1,2:T(8,128)(2,1)S(1)}, u32[]{:S(2)}, u32[]{:S(2)}) async-start(bf16[48,4,8,256]{3,0,1,2:T(8,128)(2,1)} %copy.89), calls=%async_computation.3 | async-start | bytes 1572864 | tf_op jit(solution)/shard_map/all_to_all | solution.py:108
  460.4 189.4 %all-to-all-start.4 = ((f32[2,4,256,2048]{3,2,0,1:T(8,128)}), f32[2,4,256,2048]{3,2,0,1:T(8,128)}, u32[]{:S(2)}, u32[]{:S(2)}) async-start(f32[2,4,256,2048]{3,2,0,1:T(8,128)} %copy.91), calls=%async_computation.4 | async-start | bytes 33554432 | tf_op jit(solution)/shard_map/all_to_all | solution.py:146
  683.3 12.8 copy-start
  760.9 18.5 %copy-start.3 = (f32[256,64,128]{2,1,0:T(8,128)S(1)}, f32[256,64,128]{2,1,0:T(8,128)}, u32[]{:S(2)}) copy-start(f32[256,64,128]{2,1,0:T(8,128)} %get-tuple-element.195) | copy-start | bytes 25165828
  760.9 31.5 %slice-start.2 = ((s8[8388608]{0:T(1024)(128)(4,1)}), s8[4194304]{0:T(1024)(128)(4,1)S(1)}, s32[]{:S(2)}) async-start(s8[8388608]{0:T(1024)(128)(4,1)} %bitcast.122), calls=%async_computation.9 | async-start | bytes 8388608
  779.4 13.0 slice-start.3
  841.0 8.4 copy-start.4
  1439.8 12.7 copy-start.1
  1502.5 18.6 %copy-start.2 = (f32[256,64,128]{2,1,0:T(8,128)S(1)}, f32[256,64,128]{2,1,0:T(8,128)}, u32[]{:S(2)}) copy-start(f32[256,64,128]{2,1,0:T(8,128)} %get-tuple-element.193) | copy-start | bytes 25165828
  1502.5 31.6 %slice-start = ((s8[8388608]{0:T(1024)(128)(4,1)}), s8[4194304]{0:T(1024)(128)(4,1)S(1)}, s32[]{:S(2)}) async-start(s8[8388608]{0:T(1024)(128)(4,1)} %bitcast.120), calls=%async_computation.7 | async-start | bytes 8388608
  1521.1 13.0 slice-start.1
  1582.7 8.4 copy-start.5
where the time goes:
time: 1620 us; the launch traced here: 1610 us
  blocking collectives  555 us (34%)
  matrix products  347 us (21%)
  other arithmetic  276 us (17%)
  waiting for transfers between devices  217 us (13%)
  local copies, waits for them, and re-layouts  194 us (12%)
  starting transfers between devices  25.2 us (2%)
    all_to_all x1, blocking collectives, on_device(): lax.all_to_all(lax.all_to_all(sectioned, 'au', split_axis=1, concat_axis=...  368 us
    all_to_all x1, blocking collectives, on_device(): lax.all_to_all(sectioned, 'au', split_axis=1, concat_axis=4, tiled=True)  187 us
    all_to_all x1, waiting for transfers between devices, on_device(): lax.all_to_all(grid, 'au', split_axis=1, concat_axis=3, tiled=True)  182 us
    dot_general x4, other arithmetic, grid_block(): return acc + jnp.dot(v_matrix, u_matrix, preferred_element_type=jnp.float32)  139 us
    add x8, other arithmetic, band_matrix(): matrix = matrix + jnp.where(gap == tap_index, weight_of(tap_index), zero)  115 us
    dot_general x4, matrix products, grid_block(): return acc + jnp.dot(v_matrix, u_matrix, preferred_element_type=jnp.float32)  101 us
    dot_general x4, matrix products, complex_einsum(): jnp.einsum(form, left_re, right_re, precision=highest)  77.8 us
    dot_general x4, matrix products, complex_einsum(): jnp.einsum(form, left_im, right_im, precision=highest)  62.5 us
  transfers between devices with their start and end apart: 5, of which 4 were waited for; matrix products, arithmetic and copies ran while one was open for 1% of the time, Pallas kernels for 0%

commit v1 on v0

v1 whole, which is shorter than its diff:
```python
import functools
import math

import jax
import jax.numpy as jnp
from jax import lax
from jax.experimental import pallas as pl
from jax.experimental.pallas import tpu as pltpu
from jax.sharding import PartitionSpec as P

GRID = 8192
TAPS = 16
LANES = 128
LOW = 64
STEP_BLOCKS = 4
FIELDS = 40
ROWS_OUT = 8


def phase_table(left, right, modulus):
    product = left[:, None] * right[None, :] % modulus
    angle = product.astype(jnp.float32) * (2.0 * math.pi / modulus)
    return jnp.cos(angle), jnp.sin(angle)


def rotated(taps, shift):
    tap = jnp.arange(TAPS, dtype=jnp.int32)[:, None]
    turned = jnp.zeros_like(taps)
    for t in range(TAPS):
        turned = turned + jnp.where((shift[None, :] + t) % TAPS == tap, taps[t : t + 1], 0)
    return turned


def tile_spread_kernel(first_ref, last_ref, pay_ref, low_ref, high_ref, acc_ref, *, tile, tiles, rows, period):
    source = pl.program_id(0)

    @pl.when(source == 0)
    def _():
        def clear(n, carry):
            acc_ref[n] = jnp.zeros(acc_ref.shape[1:], jnp.float32)
            return carry

        lax.fori_loop(0, acc_ref.shape[0], clear, 0)

    tap = lax.broadcasted_iota(jnp.int32, (TAPS, tile), 0).astype(jnp.float32)
    step_cells = STEP_BLOCKS * LANES

    def one_tile(t, carry):
        lanes = pl.ds(pl.multiple_of(t * tile, tile), tile)
        taps_v = pay_ref[0, 0:TAPS, lanes]
        taps_u = pay_ref[0, TAPS : 2 * TAPS, lanes]
        extra = pay_ref[0, 2 * TAPS : 2 * TAPS + 8, lanes].astype(jnp.float32)
        col_sixteenth = extra[0:1] * 16.0 + extra[1:2]
        col_low = extra[2:3]
        row_high = extra[3:4].astype(jnp.bfloat16)
        row_sixteenth = extra[4:5]
        row_low = extra[5:6]
        vis_re = extra[6:7].astype(jnp.bfloat16)
        vis_im = extra[7:8].astype(jnp.bfloat16)
        zero = jnp.zeros((), jnp.bfloat16)
        spot_u = (row_sixteenth + jnp.where(tap < row_low, 1.0, 0.0)).astype(jnp.bfloat16)
        band_u = jnp.concatenate(
            [jnp.where(spot_u == jnp.bfloat16(q), taps_u, zero) for q in range(LOW // TAPS + 1)], axis=0
        )
        low = jnp.dot(low_ref[...], band_u, preferred_element_type=jnp.float32)
        high_count = GRID // LOW
        number = lax.broadcasted_iota(jnp.int32, (high_count, tile), 0).astype(jnp.float32).astype(jnp.bfloat16)
        here = number == jnp.broadcast_to(row_high, (high_count, tile))
        picked = jnp.concatenate(
            [
                jnp.where(here, jnp.broadcast_to(vis_re, (high_count, tile)), zero),
                jnp.where(here, jnp.broadcast_to(vis_im, (high_count, tile)), zero),
            ],
            axis=0,
        )
        high = jnp.dot(high_ref[...], picked, preferred_element_type=jnp.float32)
        high_re, high_im = high[:period], high[period:]
        parts_re, parts_im = [], []
        for begin in range(0, rows, period):
            low_re = low[begin : begin + period]
            low_im = low[rows + begin : rows + begin + period]
            parts_re.append((low_re * high_re - low_im * high_im).astype(jnp.bfloat16))
            parts_im.append((low_re * high_im + low_im * high_re).astype(jnp.bfloat16))
        spread = jnp.concatenate(parts_re + parts_im, axis=0)
        spot_v = col_sixteenth + jnp.where(tap < col_low, 1.0, 0.0)

        def one_step(block, carry):
            base = (block * (step_cells // TAPS)).astype(jnp.float32)
            near = jnp.clip(spot_v - base, -1.0, step_cells / TAPS).astype(jnp.bfloat16)
            band_v = jnp.concatenate(
                [jnp.where(near == jnp.bfloat16(q), taps_v, zero) for q in range(step_cells // TAPS)], axis=0
            )
            out = lax.dot_general(spread, band_v, (((1,), (1,)), ((), ())), preferred_element_type=jnp.float32)
            for j in range(STEP_BLOCKS):
                acc_ref[block * STEP_BLOCKS + j] += out[:, j * LANES : (j + 1) * LANES]
            return carry

        place = source * tiles + t
        lax.fori_loop(first_ref[place], last_ref[place] + 1, one_step, 0)
        return carry

    lax.fori_loop(0, tiles, one_tile, 0)


def row_transform_kernel(plane_ref, first_ref, cos_ref, sin_ref, second_ref, out_ref):
    length = plane_ref.shape[0]
    stack = jnp.concatenate(
        [
            jnp.concatenate([plane_ref[:, part, m, :] for m in range(ROWS_OUT)], axis=1)
            for part in range(2)
        ],
        axis=0,
    ).astype(jnp.bfloat16)
    mid = jnp.dot(first_ref[...], stack, preferred_element_type=jnp.float32)
    cos, sin = cos_ref[...], sin_ref[...]
    rows = []
    for m in range(ROWS_OUT):
        re = mid[:length, m * LANES : (m + 1) * LANES]
        im = mid[length:, m * LANES : (m + 1) * LANES]
        rows.append(
            jnp.concatenate(
                [(re * cos - im * sin).astype(jnp.bfloat16), (re * sin + im * cos).astype(jnp.bfloat16)], axis=1
            )
        )
    turned = jnp.concatenate(rows, axis=0)
    out = lax.dot_general(second_ref[...], turned, (((1,), (1,)), ((), ())), preferred_element_type=jnp.float32)
    half = LANES // 2
    left = lax.broadcasted_iota(jnp.int32, (half, LANES), 1) < half
    for part in range(2):
        for pair in range(ROWS_OUT // 2):
            lanes = slice(pair * LANES, (pair + 1) * LANES)
            even = out[2 * part * half : (2 * part + 1) * half, lanes]
            odd = out[(2 * part + 1) * half : (2 * part + 2) * half, lanes]
            out_ref[part, 2 * pair] = jnp.where(left, even, pltpu.roll(odd, half, 1))
            out_ref[part, 2 * pair + 1] = jnp.where(left, pltpu.roll(even, half, 1), odd)


def stacked(cos, sin):
    return jnp.concatenate(
        [jnp.concatenate([cos, -sin], axis=1), jnp.concatenate([sin, cos], axis=1)], axis=0
    ).astype(jnp.bfloat16)


def on_device(visibility, taps_u, taps_v, facet, u_offset, v_offset):
    n_au = lax.axis_size("au")
    n_vert = lax.axis_size("vert")
    devices = n_au * n_vert
    count = visibility.shape[1]
    rows = GRID // devices
    own = lax.axis_index("au") * n_vert + lax.axis_index("vert")
    target = facet[:, 0]
    row = target // n_vert * (GRID // n_au) + u_offset
    col = target % n_vert * (GRID // n_vert) + v_offset
    key = col * count + jnp.arange(count, dtype=jnp.int32)
    rank = jnp.sum((key[:, None] < key[None, :]).astype(jnp.int32), axis=0)
    scalars = jnp.stack(
        [col // 256, col % 256 // TAPS, col % TAPS, row // LOW, row % LOW // TAPS, row % TAPS]
    ).astype(jnp.bfloat16)
    payload = jnp.concatenate(
        [rotated(taps_v, col % TAPS), rotated(taps_u, row % TAPS), scalars, visibility], axis=0
    )
    order = (rank[:, None] == jnp.arange(count, dtype=jnp.int32)[None, :]).astype(jnp.bfloat16)
    payload = jnp.dot(payload, order, preferred_element_type=jnp.float32).astype(jnp.bfloat16)
    gathered = lax.all_gather(payload, ("au", "vert"), axis=0)
    tile = math.gcd(count, 256)
    tiles = count // tile
    ends = gathered[:, 2 * TAPS : 2 * TAPS + 3, :].astype(jnp.int32)
    columns = (ends[:, 0] * 256 + ends[:, 1] * TAPS + ends[:, 2]).reshape(devices * tiles, tile)
    step_cells = STEP_BLOCKS * LANES
    first = jnp.min(columns, axis=1) // step_cells
    last = (jnp.max(columns, axis=1) + TAPS - 1) // step_cells

    k = own * rows + jnp.arange(rows, dtype=jnp.int32)
    low_cos, low_sin = phase_table(k, jnp.arange(LOW + TAPS, dtype=jnp.int32), GRID)
    low_table = jnp.concatenate([low_cos, low_sin], axis=0).astype(jnp.bfloat16)
    high_count = GRID // LOW
    period = min(rows, high_count)
    high_table = stacked(*phase_table(k[:period], jnp.arange(high_count, dtype=jnp.int32), high_count))
    blocks = GRID // LANES
    plane = pl.pallas_call(
        functools.partial(tile_spread_kernel, tile=tile, tiles=tiles, rows=rows, period=period),
        grid_spec=pltpu.PrefetchScalarGridSpec(
            num_scalar_prefetch=2,
            grid=(devices,),
            in_specs=[
                pl.BlockSpec((1, FIELDS, count), lambda s, *_: (s, 0, 0)),
                pl.BlockSpec(low_table.shape, lambda s, *_: (0, 0)),
                pl.BlockSpec(high_table.shape, lambda s, *_: (0, 0)),
            ],
            out_specs=pl.BlockSpec((blocks, 2 * rows, LANES), lambda s, *_: (0, 0, 0)),
        ),
        out_shape=jax.ShapeDtypeStruct((blocks, 2 * rows, LANES), jnp.float32),
        compiler_params=pltpu.CompilerParams(vmem_limit_bytes=60 * 1024 * 1024),
    )(first, last, gathered, low_table, high_table)

    a = jnp.arange(blocks, dtype=jnp.int32)
    b = jnp.arange(LANES, dtype=jnp.int32)
    first_table = stacked(*phase_table(a, a, blocks))
    cos, sin = phase_table(a, b, GRID)
    scale = 1.0 / math.sqrt(count * devices)
    mu = jnp.concatenate([jnp.arange(0, LANES, 2, dtype=jnp.int32), jnp.arange(1, LANES, 2, dtype=jnp.int32)])
    second_table = stacked(*phase_table(mu, b, LANES))
    whole = lambda shape: pl.BlockSpec(shape, lambda n: (0,) * len(shape))
    picture = pl.pallas_call(
        row_transform_kernel,
        grid=(rows // ROWS_OUT,),
        in_specs=[
            pl.BlockSpec((blocks, 2, ROWS_OUT, LANES), lambda n: (0, 0, n, 0)),
            whole(first_table.shape),
            whole(cos.shape),
            whole(sin.shape),
            whole(second_table.shape),
        ],
        out_specs=pl.BlockSpec((2, ROWS_OUT, blocks, LANES), lambda n: (0, n, 0, 0)),
        out_shape=jax.ShapeDtypeStruct((2, rows, blocks, LANES), jnp.float32),
        compiler_params=pltpu.CompilerParams(vmem_limit_bytes=48 * 1024 * 1024),
    )(plane.reshape(blocks, 2, rows, LANES), first_table, cos * scale, sin * scale, second_table)
    return picture.reshape(2, rows, GRID)


def solution(mesh):
    return jax.shard_map(
        on_device,
        mesh=mesh,
        in_specs=(
            P(None, ("au", "vert")),
            P(None, ("au", "vert")),
            P(None, ("au", "vert")),
            P(("au", "vert"), None),
            P(("au", "vert")),
            P(("au", "vert")),
        ),
        out_specs=P(None, ("au", "vert"), None),
        check_vma=False,
    )
```

time: 1620 us -> 477 us (0.29)
  blocking collectives: 555 us -> 0 us
  Pallas kernels: 0 us -> 361 us
  matrix products: 347 us -> 4.05 us
  other arithmetic: 276 us -> 10.3 us
  local copies, waits for them, and re-layouts: 194 us -> 22.3 us
  waiting for transfers between devices: 217 us -> 64.9 us
  starting transfers between devices: 25.2 us -> 0.01 us
    all_to_all x2 -> x0, blocking collectives: 555 us -> none  [the longest x1 368 us: on_device(): lax.all_to_all(lax.all_to_all(sectioned, 'au', split_axis=1, concat_axis=...]
    pallas_call x0 -> x2, Pallas kernels: none -> 361 us  [the longest x1 327 us: on_device(): pl.pallas_call(functools.partial(tile_spread_kernel, tile=tile, tiles=til...]
    dot_general x20 -> x1, matrix products: 347 us -> 4.05 us  [on_device(): jnp.dot(payload, order, preferred_element_type=jnp.float32)]
    all_to_all x5 -> x0, waiting for transfers between devices: 217 us -> none  [the longest x1 182 us: on_device(): lax.all_to_all(grid, 'au', split_axis=1, concat_axis=3, tiled=True)]
    dot_general x4 -> x0, other arithmetic: 139 us -> none  [grid_block(): return acc + jnp.dot(v_matrix, u_matrix, preferred_element_type=jnp.float32)]
    add x9 -> x4, other arithmetic: 116 us -> 1.72 us  [the longest x1 1.11 us: on_device(): ends[:, 0] * 256 + ends[:, 1] * TAPS + ends[:, 2]]
    all_gather x0 -> x1, waiting for transfers between devices: none -> 64.9 us  [on_device(): gathered = lax.all_gather(payload, ('au', 'vert'), axis=0)]
    slice x16 -> x3, local copies, waits for them, and re-layouts: 46.9 us -> 3.24 us  [the longest x2 3.23 us: rotated(): taps[t:t + 1]]
  transfers between devices with their start and end apart: 5 -> 1, of which waited for: 4 -> 1; matrix products, arithmetic and copies ran while one was open for 1% -> 1% of each run, Pallas kernels for 0% -> 0%
where the time goes in v1:
time: 477 us; the launch traced here: 476 us
  Pallas kernels  361 us (76%)
  waiting for transfers between devices  64.9 us (14%)
  local copies, waits for them, and re-layouts  22.3 us (5%)
  between operations  13.6 us (3%)
  other arithmetic  10.3 us (2%)
    pallas_call x1, Pallas kernels, on_device(): pl.pallas_call(functools.partial(tile_spread_kernel, tile=tile, tiles=til...  327 us
    all_gather x1, waiting for transfers between devices, on_device(): gathered = lax.all_gather(payload, ('au', 'vert'), axis=0)  64.9 us
    pallas_call x1, Pallas kernels, on_device(): pl.pallas_call(row_transform_kernel, grid=(rows // ROWS_OUT,), in_specs=[...  33.5 us
    reshape x1, local copies, waits for them, and re-layouts, on_device(): return picture.reshape(2, rows, GRID)  18.2 us
  transfers between devices with their start and end apart: 1, of which 1 were waited for; matrix products, arithmetic and copies ran while one was open for 1% of the time, Pallas kernels for 0%

profile of v1, /device:TPU:0, one launch (start us, length us, event | category | flops | bytes accessed | tf_op | source)
XLA Modules:
  0.0 475.7 jit_solution(7884730732262496450)
XLA Ops:
  6.5 0.0 all-gather.3.cloned.1.call-start
  6.5 0.8 fusion.154
  7.3 1.7 convert_reduce_fusion
  9.0 1.6 slice_reduce_fusion.15
  10.6 1.6 slice_reduce_fusion.31
  12.3 0.2 fusion.144
  12.5 0.3 fusion.64
  12.8 0.3 fusion.49
  13.1 0.8 concatenate.47
  13.9 4.0 fusion.2
  18.0 0.0 all-gather.3.cloned.1.call-update
  18.0 0.1 pad_add_fusion
  18.1 0.1 fusion.102
  18.2 0.2 negate_convert_fusion.2
  18.4 0.1 maximum_maximum_fusion.2.first_ref
  18.5 0.2 sine_multiply_fusion
  18.7 0.6 cosine_convert_fusion
  19.3 0.7 pad_maximum_fusion.low_ref
  19.9 0.3 negate_convert_fusion
  20.3 0.3 negate_convert_fusion.1
  20.7 0.7 maximum_maximum_fusion.high_ref
  21.3 64.9 %all-gather.3.cloned.1.call-done = bf16[1280,2048]{1,0:T(8,128)(2,1)} async-done(((bf16[40,2048]{1,0:T(8,128)(2,1)}), bf16[1280,2048]{1,0:T(8,128)(2,1)}) %all-gather.3.cloned.1.call-update) | async-done | bytes 5242896 | tf_op jit(solution)/shard_map/all_gather | solution.py:164
  86.2 1.4 slice_convert_fusion
  87.6 1.1 fusion.3
  88.8 0.1 fusion.155
  88.9 0.6 and_select_fusion.last_ref
  89.5 0.6 and_select_fusion.1.first_ref
  90.1 327.0 %shard_map.64 = f32[64,512,128]{2,1,0:T(8,128)} custom-call(s32[256]{0:T(256)} %and_select_fusion.1.first_ref, s32[256]{0:T(256)} %and_select_fusion.last_ref, bf16[32,40,2048]{2,1,0:T(8,128)(2,1)} %bitcast.8, bf16[512,80]{1,0:T(8,128)(2,1)} %pad_maximum_fusion.low_ref, bf16[256,256]{1,0:T(8,128)(2,1)} %maximum_maximum_fusion.high_ref), custom_call_target="tpu_custom_call" | custom-call | tf_op jit(solution)/shard_map/pallas_call | solution.py:180
  417.2 33.5 %shard_map.65 = f32[2,256,64,128]{3,2,1,0:T(8,128)} custom-call(f32[64,2,256,128]{3,2,1,0:T(8,128)} %bitcast.6, bf16[128,128]{1,0:T(8,128)(2,1)S(1)} %maximum_maximum_fusion.2.first_ref, f32[64,128]{1,0:T(8,128)S(1)} %get-tuple-element.114.cos_ref, f32[64,128]{1,0:T(8,128)S(1)} %get-tuple-element.113.sin_ref, ...), custom_call_target="tpu_custom_call" | custom-call | tf_op jit(solution)/shard_map/pallas_call | solution.py:204
  450.7 18.2 %reshape.280 = f32[2,256,8192]{2,1,0:T(8,128)} reshape(f32[2,256,64,128]{3,2,1,0:T(8,128)} %shard_map.65) | data formatting | bytes 33554432 | tf_op jit(solution)/shard_map/reshape | solution.py:218
  (11 shorter events, 0.1 us)
Async XLA Ops:
  6.5 79.7 %all-gather.3.cloned.1.call-start = ((), (), s32[]{:S(2)}) async-start(), calls=%async_computation | async-start | bytes 5406720 | tf_op jit(solution)/shard_map/all_gather | solution.py:164
Sparse Core Ops, SparseCore 0:
  18.1 68.0 all-gather.2
